TPU v7x, 32 devices: a whole 2x2x4 slice. The times are simulated.
32 devices in a mesh: outer: 4 (over y, core), row: 4 (over z), col: 2 (over x).
Axes of the slice: x: 2, y: 2, z: 4, core: 2. Of those that a mesh axis runs over, the one named last changes fastest.
Arguments:
- activations: bfloat16 [2048, 9216], P(('outer', 'col'), 'row'), may hold values from -13 to 13
- out_grads: bfloat16 [2048, 8192], P(('outer', 'row'), 'col'), may hold values from -13 to 13
- row_moment: float32 [9216], P(('row', 'outer')), may hold values from 0.3 to 3
- col_moment: float32 [8192], P('col'), may hold values from 0.3 to 3
Outputs:
- update: bfloat16 [9216, 8192], P(('row', 'outer'), 'col')
- new_row: float32 [9216], P(('row', 'outer'))
- new_col: float32 [8192], P('col')
All inputs are finite; a program needn't handle non-finite values.
Results may differ from a plain program's by a relative error of at most 0.001.
Values may be sent and summed in bfloat16 or wider, within the bound.
A program may use at most 128 MiB of HBM per device.

v0:
```python
import jax
import jax.numpy as jnp
from jax import lax
from jax.sharding import PartitionSpec as P

D = 9216
F = 8192
STEP = 2


def body(activations, out_grads, row_moment, col_moment):
    row_count = row_moment.shape[0]
    quarter = lax.axis_index("outer") * row_count
    token_count = activations.shape[0] * lax.axis_size("col") * lax.axis_size("outer")
    contract = (((0,), (0,)), ((), ()))
    grads_all = lax.all_gather(out_grads, ("outer", "row"), axis=0, tiled=True)
    columns = lax.dynamic_slice_in_dim(
        lax.all_gather(activations, ("outer", "col"), axis=0, tiled=True), quarter, row_count, 1
    )
    gradient = lax.dot_general(columns, grads_all, contract, preferred_element_type=jnp.float32)
    gradient = gradient * (1.0 / token_count**0.5)
    squares = gradient * gradient
    col_squares, old_total = lax.psum(
        (jnp.sum(squares, axis=0), jnp.sum(row_moment)), ("outer", "row")
    )
    row_squares, grad_total = lax.psum((jnp.sum(squares, axis=1), jnp.sum(col_squares)), "col")
    decay_rate = 1.0 - STEP ** (-0.8)
    new_row = decay_rate * row_moment + (1.0 - decay_rate) * row_squares / F
    new_col = decay_rate * col_moment + (1.0 - decay_rate) * col_squares / D
    moment_total = decay_rate * old_total + (1.0 - decay_rate) * grad_total / F
    factor = lax.rsqrt(new_row[:, None] * new_col[None, :] * (D / moment_total))
    update = (gradient * factor).astype(jnp.bfloat16)
    return (update, new_row, new_col)


def solution(mesh):
    return jax.shard_map(
        body,
        mesh=mesh,
        in_specs=(
            P(("outer", "col"), "row"),
            P(("outer", "row"), "col"),
            P(("row", "outer")),
            P("col"),
        ),
        out_specs=(P(("row", "outer"), "col"), P(("row", "outer")), P("col")),
        check_vma=False,
    )
```

profile of v0, /device:TPU:0, one launch (start us, length us, event | category | flops | bytes accessed | tf_op | source)
XLA Modules:
  0.0 298.9 jit_solution(16557002799071541110)
XLA Ops:
  7.2 0.0 all-gather.3.cloned.1.call-start
  7.2 0.7 all-gather.3.cloned.1.call-update
  7.9 0.0 all-gather.5.cloned.1.call-start
  7.9 0.7 all-gather.5.cloned.1.call-update
  8.7 1.3 reduce_sum.38
  9.9 0.0 copy-start.1
  9.9 0.0 copy-start.2
  10.0 61.4 %all-gather.3.cloned.1.call-done = bf16[2048,2304]{1,0:T(8,128)(2,1)} async-done(((bf16[256,2304]{1,0:T(8,128)(2,1)}), bf16[2048,2304]{1,0:T(8,128)(2,1)}) %all-gather.3.cloned.1.call-update) | async-done | bytes 9437200 | tf_op jit(solution)/shard_map/all_gather | solution.py:18
  71.3 128.7 %all-gather.5.cloned.1.call-done = bf16[2048,4096]{1,0:T(8,128)(2,1)} async-done(((bf16[128,4096]{1,0:T(8,128)(2,1)}), bf16[2048,4096]{1,0:T(8,128)(2,1)}) %all-gather.5.cloned.1.call-update) | async-done | bytes 16777232 | tf_op jit(solution)/shard_map/all_gather | solution.py:16
  200.0 17.7 %multiply_reduce_fusion.1 = (f32[576]{0:T(1024)S(1)}, f32[4096]{0:T(1024)S(1)}, f32[576,4096]{1,0:T(8,128)}) fusion(bf16[2048,4096]{1,0:T(8,128)(2,1)} %all-gather.5.cloned.1.call-done, bf16[2048,2304]{1,0:T(8,128)(2,1)} %all-gather.3.cloned.1.call-done, s32[]{:T(128)S(6)} %select_n.3), kind=kOutput, calls=%fused_computation.2 | convolution fusion | flops 9673108480 | bytes 28854532 | tf_op jit(solution)/shard_map/dot_general | solution.py:20
  217.7 58.9 %all-reduce = (f32[]{:T(128)}, f32[4096]{0:T(1024)S(1)}) all-reduce(f32[]{:T(128)} %reduce_sum.38, f32[4096]{0:T(1024)S(1)} %get-tuple-element.4), channel_id=1, replica_groups=mesh['outer'=4,'row'=4,'col'=2] {'outer','row'}, use_global_device_ids=true, to_apply=%region_5.0 | all-reduce | flops 4097 | bytes 32776 | tf_op jit(solution)/shard_map/psum | solution.py:23
  276.6 0.0 copy-done.1
  276.6 0.6 multiply_add_fusion
  277.2 0.0 copy-start
  277.2 5.7 %all-reduce.1 = (f32[]{:T(128)}, f32[576]{0:T(1024)S(1)}) all-reduce(f32[]{:T(128)} %get-tuple-element.10, f32[576]{0:T(1024)S(1)} %get-tuple-element.3), channel_id=1, replica_groups=mesh['outer'=4,'row'=4,'col'=2] {'col'}, use_global_device_ids=true, to_apply=%region_7.0 | all-reduce | flops 577 | bytes 4616 | tf_op jit(solution)/shard_map/psum | solution.py:26
  282.9 0.0 copy-done.2
  282.9 0.0 copy-start.3
  284.3 7.8 %multiply_convert_fusion = bf16[576,4096]{1,0:T(8,128)(2,1)} fusion(f32[576,4096]{1,0:T(8,128)} %get-tuple-element.11, f32[]{:T(128)S(6)} %div.23, f32[4096]{0:T(1024)S(1)} %get-tuple-element.9, f32[576]{0:T(1024)S(1)} %multiply_add_fusion.1), kind=kLoop, calls=%fused_computation | loop fusion | flops 11796480 | bytes 14174468 | tf_op jit(solution)/shard_map/convert_element_type | solution.py:32
  292.0 0.0 copy-done
  292.0 0.0 copy-done.3
  (1 shorter events, 0.0 us)
Async XLA Ops:
  7.2 64.1 %all-gather.3.cloned.1.call-start = ((), (), s32[]{:S(2)}) async-start(), calls=%async_computation | async-start | bytes 10616832 | tf_op jit(solution)/shard_map/all_gather | solution.py:18
  7.9 192.1 %all-gather.5.cloned.1.call-start = ((), (), s32[]{:S(2)}) async-start(), calls=%async_computation.1 | async-start | bytes 17825792 | tf_op jit(solution)/shard_map/all_gather | solution.py:16
  9.9 266.6 %copy-start.1 = (f32[4096]{0:T(1024)S(1)}, f32[4096]{0:T(1024)}, u32[]{:S(2)}) copy-start(f32[4096]{0:T(1024)} %param.7) | copy-start | bytes 49156
  9.9 272.9 %copy-start.2 = (f32[576]{0:T(1024)S(1)}, f32[576]{0:T(1024)}, u32[]{:S(2)}) copy-start(f32[576]{0:T(1024)} %param.6) | copy-start | bytes 6916
  277.2 14.9 %copy-start = (f32[4096]{0:T(1024)}, f32[4096]{0:T(1024)S(1)}, u32[]{:S(2)}) copy-start(f32[4096]{0:T(1024)S(1)} %get-tuple-element.9) | copy-start | bytes 49156
  282.9 9.2 %copy-start.3 = (f32[576]{0:T(1024)}, f32[576]{0:T(1024)S(1)}, u32[]{:S(2)}) copy-start(f32[576]{0:T(1024)S(1)} %multiply_add_fusion.1) | copy-start | bytes 6916
Sparse Core Ops, SparseCore 0:
  9.9 61.4 all-gather.2
  73.5 126.4 all-gather.4
where the time goes:
time: 299 us
  waiting for transfers between devices  191 us (64%)
  blocking collectives  64.5 us (22%)
  matrix products  17.7 us (6%)
  between operations  15.4 us (5%)
  other arithmetic  9.68 us (3%)
    all_gather x1, waiting for transfers between devices, body(): grads_all = lax.all_gather(out_grads, ('outer', 'row'), axis=0, tiled=True)  129 us
    all_gather x1, waiting for transfers between devices, body(): lax.all_gather(activations, ('outer', 'col'), axis=0, tiled=True)  61.4 us
    psum x1, blocking collectives, body(): lax.psum((jnp.sum(squares, axis=0), jnp.sum(row_moment)), ('outer', 'row'))  58.9 us
    dot_general x1, matrix products, body(): lax.dot_general(columns, grads_all, contract, preferred_element_type=jnp....  17.7 us
    convert_element_type x1, other arithmetic, body(): update = (gradient * factor).astype(jnp.bfloat16)  7.78 us
  transfers between devices with their start and end apart: 2, of which 2 were waited for; matrix products, arithmetic and copies ran while one was open for 0% of the time, Pallas kernels for 0%

commit v1 on v0

--- a/solution.py
+++ b/solution.py
@@ -15,7 +15,15 @@
     contract = (((0,), (0,)), ((), ()))
     grads_all = lax.all_gather(out_grads, ("outer", "row"), axis=0, tiled=True)
     columns = lax.dynamic_slice_in_dim(
-        lax.all_gather(activations, ("outer", "col"), axis=0, tiled=True), quarter, row_count, 1
+        jnp.concatenate(
+            lax.all_to_all(
+                jnp.stack([activations] * lax.axis_size(("outer", "col"))), ("outer", "col"), 0, 0
+            ),
+            axis=0,
+        ),
+        quarter,
+        row_count,
+        1,
     )
     gradient = lax.dot_general(columns, grads_all, contract, preferred_element_type=jnp.float32)
     gradient = gradient * (1.0 / token_count**0.5)

time: 299 us -> 309 us (1.033)
  local copies, waits for them, and re-layouts: 0.01 us -> 5.52 us
  starting transfers between devices: 0.08 us -> 5.37 us
    all_to_all x0 -> x1, waiting for transfers between devices: none -> 142 us  [body(): lax.all_to_all(jnp.stack([activations] * lax.axis_size(('outer', 'col')))...]
    all_gather x1, waiting for transfers between devices: 129 us -> 48.4 us  [body(): grads_all = lax.all_gather(out_grads, ('outer', 'row'), axis=0, tiled=True)]
    all_gather x1 -> x0, waiting for transfers between devices: 61.4 us -> none  [body(): lax.all_gather(activations, ('outer', 'col'), axis=0, tiled=True)]
    another operation x0 -> x1, local copies, waits for them, and re-layouts: none -> 5.5 us  [body(): jnp.stack([activations] * lax.axis_size(('outer', 'col')))]
    all_to_all x0 -> x1, starting transfers between devices: none -> 5.33 us  [body(): lax.all_to_all(jnp.stack([activations] * lax.axis_size(('outer', 'col')))...]
  transfers between devices with their start and end apart: 2 -> 2, of which waited for: 2 -> 2; matrix products, arithmetic and copies ran while one was open for 0% -> 2% of each run, Pallas kernels for 0% -> 0%
where the time goes in v1:
time: 309 us; the launch traced here: 308 us
  waiting for transfers between devices  191 us (62%)
  blocking collectives  64.5 us (21%)
  matrix products  17.8 us (6%)
  between operations  15.4 us (5%)
  other arithmetic  8.99 us (3%)
  local copies, waits for them, and re-layouts  5.52 us (2%)
  starting transfers between devices  5.37 us (2%)
    all_to_all x1, waiting for transfers between devices, body(): lax.all_to_all(jnp.stack([activations] * lax.axis_size(('outer', 'col')))...  142 us
    psum x1, blocking collectives, body(): lax.psum((jnp.sum(squares, axis=0), jnp.sum(row_moment)), ('outer', 'row'))  58.8 us
    all_gather x1, waiting for transfers between devices, body(): grads_all = lax.all_gather(out_grads, ('outer', 'row'), axis=0, tiled=True)  48.4 us
    dot_general x1, matrix products, body(): lax.dot_general(columns, grads_all, contract, preferred_element_type=jnp....  17.8 us
    convert_element_type x1, other arithmetic, body(): update = (gradient * factor).astype(jnp.bfloat16)  7.78 us
  transfers between devices with their start and end apart: 2, of which 2 were waited for; matrix products, arithmetic and copies ran while one was open for 2% of the time, Pallas kernels for 0%

profile of v1, /device:TPU:0, one launch (start us, length us, event | category | flops | bytes accessed | tf_op | source)
XLA Modules:
  0.0 308.2 jit_solution(5789355104361110629)
XLA Ops:
  7.2 0.0 all-gather.2.cloned.1.call-start
  7.2 0.7 all-gather.2.cloned.1.call-update
  7.9 5.5 %stack.2 = bf16[8,256,2304]{2,1,0:T(8,128)(2,1)} broadcast(bf16[256,2304]{1,0:T(8,128)(2,1)} %param.4), dimensions={1,2} | broadcast | bytes 10616832 | tf_op jit(solution)/shard_map/stack | solution.py:20
  13.4 0.0 copy-start.2
  13.4 5.3 %all-to-all-start = ((bf16[8,256,2304]{2,1,0:T(8,128)(2,1)}), bf16[8,256,2304]{2,1,0:T(8,128)(2,1)}, u32[]{:S(2)}, u32[]{:S(2)}) async-start(bf16[8,256,2304]{2,1,0:T(8,128)(2,1)} %stack.2), calls=%async_computation | async-start | bytes 18874368 | tf_op jit(solution)/shard_map/all_to_all | solution.py:19
  18.7 0.0 copy-done.2
  18.7 0.6 reduce_sum.38
  19.3 141.6 %all-to-all-done = bf16[8,256,2304]{2,1,0:T(8,128)(2,1)} async-done(((bf16[8,256,2304]{2,1,0:T(8,128)(2,1)}), bf16[8,256,2304]{2,1,0:T(8,128)(2,1)}, u32[]{:S(2)}, u32[]{:S(2)}) %all-to-all-start) | async-done | bytes 9437216 | tf_op jit(solution)/shard_map/all_to_all | solution.py:19
  160.9 48.4 %all-gather.2.cloned.1.call-done = bf16[2048,4096]{1,0:T(8,128)(2,1)} async-done(((bf16[128,4096]{1,0:T(8,128)(2,1)}), bf16[2048,4096]{1,0:T(8,128)(2,1)}) %all-gather.2.cloned.1.call-update) | async-done | bytes 16777232 | tf_op jit(solution)/shard_map/all_gather | solution.py:16
  209.4 0.0 copy-start.1
  209.4 17.8 %multiply_reduce_fusion.1 = (f32[576]{0:T(1024)S(1)}, f32[4096]{0:T(1024)S(1)}, f32[576,4096]{1,0:T(8,128)}) fusion(bf16[2048,4096]{1,0:T(8,128)(2,1)} %all-gather.2.cloned.1.call-done, bf16[2048,2304]{1,0:T(8,128)(2,1)} %bitcast, s32[]{:T(128)S(6)} %select_n.3), kind=kOutput, calls=%fused_computation.2 | convolution fusion | flops 9673108480 | bytes 28854532 | tf_op jit(solution)/shard_map/dot_general | solution.py:28
  227.1 58.8 %all-reduce = (f32[]{:T(128)}, f32[4096]{0:T(1024)S(1)}) all-reduce(f32[]{:T(128)} %reduce_sum.38, f32[4096]{0:T(1024)S(1)} %get-tuple-element.4), channel_id=1, replica_groups=mesh['outer'=4,'row'=4,'col'=2] {'outer','row'}, use_global_device_ids=true, to_apply=%region_5.0 | all-reduce | flops 4097 | bytes 32776 | tf_op jit(solution)/shard_map/psum | solution.py:31
  285.9 0.0 copy-done.1
  285.9 0.6 multiply_add_fusion
  286.5 0.0 copy-start
  286.5 5.7 %all-reduce.1 = (f32[]{:T(128)}, f32[576]{0:T(1024)S(1)}) all-reduce(f32[]{:T(128)} %get-tuple-element.10, f32[576]{0:T(1024)S(1)} %get-tuple-element.3), channel_id=1, replica_groups=mesh['outer'=4,'row'=4,'col'=2] {'col'}, use_global_device_ids=true, to_apply=%region_7.0 | all-reduce | flops 577 | bytes 4616 | tf_op jit(solution)/shard_map/psum | solution.py:34
  292.2 0.0 copy-start.3
  293.6 7.8 %multiply_convert_fusion = bf16[576,4096]{1,0:T(8,128)(2,1)} fusion(f32[576,4096]{1,0:T(8,128)} %get-tuple-element.11, f32[]{:T(128)S(6)} %div.23, f32[4096]{0:T(1024)S(1)} %get-tuple-element.9, f32[576]{0:T(1024)S(1)} %multiply_add_fusion.1), kind=kLoop, calls=%fused_computation | loop fusion | flops 11796480 | bytes 14174468 | tf_op jit(solution)/shard_map/convert_element_type | solution.py:40
  301.4 0.0 copy-done
  301.4 0.0 copy-done.3
  (1 shorter events, 0.0 us)
Async XLA Ops:
  7.2 202.2 %all-gather.2.cloned.1.call-start = ((), (), s32[]{:S(2)}) async-start(), calls=%async_computation.1 | async-start | bytes 17825792 | tf_op jit(solution)/shard_map/all_gather | solution.py:16
  13.4 5.3 %copy-start.2 = (f32[576]{0:T(1024)S(1)}, f32[576]{0:T(1024)}, u32[]{:S(2)}) copy-start(f32[576]{0:T(1024)} %param.6) | copy-start | bytes 6916
  13.4 147.5 %all-to-all-start = ((bf16[8,256,2304]{2,1,0:T(8,128)(2,1)}), bf16[8,256,2304]{2,1,0:T(8,128)(2,1)}, u32[]{:S(2)}, u32[]{:S(2)}) async-start(bf16[8,256,2304]{2,1,0:T(8,128)(2,1)} %stack.2), calls=%async_computation | async-start | bytes 18874368 | tf_op jit(solution)/shard_map/all_to_all | solution.py:19
  209.4 76.6 %copy-start.1 = (f32[4096]{0:T(1024)S(1)}, f32[4096]{0:T(1024)}, u32[]{:S(2)}) copy-start(f32[4096]{0:T(1024)} %param.7) | copy-start | bytes 49156
  286.5 14.9 %copy-start = (f32[4096]{0:T(1024)}, f32[4096]{0:T(1024)S(1)}, u32[]{:S(2)}) copy-start(f32[4096]{0:T(1024)S(1)} %get-tuple-element.9) | copy-start | bytes 49156
  292.2 9.2 %copy-start.3 = (f32[576]{0:T(1024)}, f32[576]{0:T(1024)S(1)}, u32[]{:S(2)}) copy-start(f32[576]{0:T(1024)S(1)} %multiply_add_fusion.1) | copy-start | bytes 6916
Sparse Core Ops, SparseCore 0:
  10.2 199.1 all-gather.1
